TPU v7x, 128 devices: a whole 4x4x4 slice. The times are simulated.
128 devices in a mesh: res: 16 (over z, x), samp: 8 (over y, core).
Axes of the slice: x: 4, y: 4, z: 4, core: 2. Of those that a mesh axis runs over, the one named last changes fastest.
Arguments:
- coords_pred: float32 [32, 3, 49152], P('samp', None, 'res'), may hold values from -130 to 130
- coords_true: float32 [3, 49152], P(None, 'res'), may hold values from -55 to 55
- atom_kind: int32 [49152], P('res'), may hold values from 0 to 2
- partners: int32 [384, 5], P('res'), may hold values from 0 to 383, as said below
- noise_level: float32 [32], P('samp'), may hold values from 2 to 32
Outputs:
- copy_loss: float32 [32], P('samp')
- mean_loss: float32 [], replicated
- coord_grad: float32 [32, 3, 49152], P('samp', None, 'res')
Inputs may be any that keep to these rules, and one draw needn't show every extreme that they name: `partners`: slot 0 of tile g holds g; the other used slots hold distinct tiles g' with 0 < |g' - g| <= 2, and unused slots hold g again; the pairing is symmetric (g' is listed for g exactly when g is listed for g'); some tile uses all 5 slots.
All inputs are finite; a program needn't handle non-finite values.
Results may differ from a plain program's by a relative error of at most 0.0005.
Values sent between devices are 32-bit elements; how exact they have to be, the bound alone decides.
A program may use at most 64 MiB of HBM per device.

v0:
```python
import math

import jax
import jax.numpy as jnp
from jax import lax
from jax.sharding import PartitionSpec as P

precise = lax.Precision.HIGHEST
thresholds = (0.5, 1.0, 2.0, 4.0)
sigma_data = 16.0


def padded(block, sides, width):
    for axis, dim in sides:
        count = lax.axis_size(axis)
        forward = [(i, i + 1) for i in range(count - 1)]
        backward = [(target, source) for source, target in forward]
        low = lax.ppermute(
            lax.slice_in_dim(block, block.shape[dim] - width, None, axis=dim), axis, forward
        )
        high = lax.ppermute(lax.slice_in_dim(block, 0, width, axis=dim), axis, backward)
        block = jnp.concatenate([low, block, high], axis=dim)
    return block


def atom_weight(atom_kind):
    return jnp.where(atom_kind == 1, 5.0, jnp.where(atom_kind == 2, 10.0, 1.0)).astype(jnp.float32)


def atom_cutoff(atom_kind):
    return jnp.where(atom_kind == 1, 30.0, 15.0).astype(jnp.float32)


def moments(coords_pred, coords_true, weight):
    weight_sum = jnp.sum(weight)
    pred_sum = jnp.einsum("sca,a->sc", coords_pred, weight, precision=precise)
    true_sum = jnp.einsum("ca,a->c", coords_true, weight, precision=precise)
    cross = jnp.einsum("sca,da->scd", coords_pred * weight, coords_true, precision=precise)
    return (weight_sum, pred_sum, true_sum, cross)


def rotation_of(weight_sum, pred_sum, true_sum, cross):
    pred_mean = pred_sum / weight_sum
    true_mean = true_sum / weight_sum
    covariance = cross - pred_sum[:, :, None] * true_mean[None, None, :]
    frobenius = jnp.sqrt(jnp.sum(covariance * covariance, axis=(1, 2)))
    polar_factor = covariance / frobenius[:, None, None]
    for sweep_index in range(20):
        gram_matrix = jnp.einsum("sab,scb->sac", polar_factor, polar_factor, precision=precise)
        polar_factor = 1.5 * polar_factor - 0.5 * jnp.einsum(
            "sac,scd->sad", gram_matrix, polar_factor, precision=precise
        )
    return (polar_factor, pred_mean, true_mean)


def aligned_truth(rotation, pred_mean, true_mean, coords_true):
    centred = coords_true - true_mean[:, None]
    return jnp.einsum("scd,da->sca", rotation, centred, precision=precise) + pred_mean[:, :, None]


def pair_terms(own_rows, partner_rows, own_tile, partner_tiles, copies):
    tile_len = own_rows.shape[-1]
    slot_count = partner_tiles.shape[0]
    own_pred = own_rows[: 3 * copies].reshape(copies, 3, tile_len)
    own_true = own_rows[3 * copies : 3 * copies + 3]
    own_cut = own_rows[3 * copies + 3]
    far_pred = partner_rows[: 3 * copies].reshape(copies, 3, slot_count, tile_len)
    far_true = partner_rows[3 * copies : 3 * copies + 3]
    far_cut = partner_rows[3 * copies + 3]
    pred_terms = []
    true_terms = []
    for component in range(3):
        coord_gap = own_pred[:, component, None, :, None] - far_pred[:, component, :, None, :]
        pred_terms.append(coord_gap * coord_gap)
        true_gap = own_true[component][None, :, None] - far_true[component][:, None, :]
        true_terms.append(true_gap * true_gap)
    pred_dist = jnp.sqrt(pred_terms[0] + pred_terms[1] + pred_terms[2] + 1e-06)
    true_dist = jnp.sqrt(true_terms[0] + true_terms[1] + true_terms[2] + 1e-06)
    slot_used = (jnp.arange(slot_count) == 0) | (partner_tiles != own_tile)
    same_atom = jnp.arange(tile_len)[:, None] == jnp.arange(tile_len)[None, :]
    diagonal = (partner_tiles == own_tile)[:, None, None] & same_atom[None]
    usable = slot_used[:, None, None] & jnp.logical_not(diagonal)
    mask_fwd = jnp.where(usable & (true_dist < far_cut[:, None, :]), 1.0, 0.0).astype(jnp.float32)
    mask_back = jnp.where(usable & (true_dist < own_cut[None, :, None]), 1.0, 0.0).astype(
        jnp.float32
    )
    spread = jnp.abs(pred_dist - true_dist)
    score_parts = []
    slope_parts = []
    for threshold in thresholds:
        squash = jax.nn.sigmoid(threshold - spread)
        score_parts.append(squash)
        slope_parts.append(squash * (1.0 - squash))
    pair_score = 0.25 * (score_parts[0] + score_parts[1] + score_parts[2] + score_parts[3])
    pair_slope = -0.25 * (slope_parts[0] + slope_parts[1] + slope_parts[2] + slope_parts[3])
    pair_count = jnp.sum(mask_fwd)
    score_sum = jnp.sum(mask_fwd * pair_score, axis=(1, 2, 3))
    factor = (mask_fwd + mask_back) * pair_slope * jnp.sign(pred_dist - true_dist) / pred_dist
    weight_row = jnp.sum(factor, axis=(1, 3))
    pull_parts = []
    for component in range(3):
        remote = jnp.einsum("skij,skj->si", factor, far_pred[:, component], precision=precise)
        pull_parts.append(own_pred[:, component] * weight_row - remote)
    return (pair_count, score_sum, jnp.stack(pull_parts, axis=1))


def shards(coords_pred, coords_true, atom_kind, partners, noise_level):
    copies = coords_pred.shape[0]
    local_atoms = coords_pred.shape[2]
    tile_count = partners.shape[0]
    tile_len = local_atoms // tile_count
    res_rank = lax.axis_index("res")
    weight = atom_weight(atom_kind)
    cutoff = atom_cutoff(atom_kind)
    packed = jnp.concatenate(
        [coords_pred.reshape(3 * copies, local_atoms), coords_true, cutoff[None]], axis=0
    )
    window = padded(packed, (("res", 1),), local_atoms)
    first_tile = (res_rank - 1) * tile_count
    row_count = packed.shape[0]
    own_tiles = packed.reshape(row_count, tile_count, tile_len)
    far_tiles = window.reshape(row_count, -1, tile_len)
    group_size = math.gcd(tile_count, max(1, 512 // tile_len))
    group_count = tile_count // group_size

    def tile_work(own_rows, partner_rows, own_tile, partner_tiles):
        return pair_terms(own_rows, partner_rows, own_tile, partner_tiles, copies)

    mapped_work = jax.vmap(tile_work, in_axes=(0, 0, 0, 0))

    def visit_group(totals, local_ids):
        own_rows = jnp.moveaxis(jnp.take(own_tiles, local_ids, axis=1), 1, 0)
        partner_tiles = jnp.take(partners, local_ids, axis=0)
        partner_rows = jnp.moveaxis(jnp.take(far_tiles, partner_tiles - first_tile, axis=1), 1, 0)
        pair_count, score_sum, pull_group = mapped_work(
            own_rows, partner_rows, res_rank * tile_count + local_ids, partner_tiles
        )
        return (
            (totals[0] + jnp.sum(pair_count), totals[1] + jnp.sum(score_sum, axis=0)),
            pull_group,
        )

    start_totals = (jnp.float32(0.0), jnp.zeros((copies,), jnp.float32))
    group_ids = jnp.arange(tile_count, dtype=jnp.int32).reshape(group_count, group_size)
    (pair_local, score_local), pull_groups = lax.scan(visit_group, start_totals, group_ids)
    pull_tiles = pull_groups.reshape(tile_count, copies, 3, tile_len)
    pull_field = jnp.moveaxis(pull_tiles, 0, 2).reshape(copies, 3, local_atoms)
    weight_sum, pred_sum, true_sum, cross = moments(coords_pred, coords_true, weight)
    weight_sum, pred_sum, true_sum, cross = lax.psum((weight_sum, pred_sum, true_sum, cross), "res")
    rotation, pred_mean, true_mean = rotation_of(weight_sum, pred_sum, true_sum, cross)
    target = aligned_truth(rotation, pred_mean, true_mean, coords_true)
    deviation = coords_pred - target
    square_local = jnp.sum(weight * deviation * deviation, axis=(1, 2))
    square_err, score_total, pair_sum = lax.psum((square_local, score_local, pair_local), "res")
    loss_weight = (noise_level * noise_level + sigma_data * sigma_data) / (
        noise_level * sigma_data * (noise_level * sigma_data)
    )
    mean_square = square_err / (3.0 * weight_sum)
    copy_loss = loss_weight * mean_square + 1.0 - score_total / pair_sum
    copy_sum = lax.psum(jnp.sum(copy_loss), "samp")
    mean_loss = copy_sum / (copies * lax.axis_size("samp"))
    atom_total = local_atoms * lax.axis_size("res")
    grad_scale = 16.0 * atom_total
    coord_grad = grad_scale * (
        2.0 * loss_weight[:, None, None] * weight * deviation / (3.0 * weight_sum)
        - pull_field / pair_sum
    )
    return (copy_loss, mean_loss, coord_grad)


def solution(mesh):
    in_specs = (P("samp", None, "res"), P(None, "res"), P("res"), P("res", None), P("samp"))
    out_specs = (P("samp"), P(), P("samp", None, "res"))
    return jax.shard_map(shards, mesh=mesh, in_specs=in_specs, out_specs=out_specs, check_vma=False)
```

profile of v0, /device:TPU:1, one launch (start us, length us, event | category | flops | bytes accessed | tf_op | source)
XLA Modules:
  0.0 588.1 jit_solution(16663953070518789256)
XLA Ops:
  5.3 4.6 collective-permute-start
  14.0 34.7 %all-reduce.1 = (f32[4,3]{0,1:T(4,128)S(1)}, f32[]{:T(128)}, f32[3]{0:T(128)S(1)}, f32[4,3,3]{0,2,1:T(4,128)S(1)}) all-reduce(f32[4,3]{0,1:T(4,128)S(1)} %bitcast.272, f32[]{:T(128)} %get-tuple-element.263, f32[3]{0:T(128)S(1)} %convolution_bitcast_fusion, f32[4,3,3]{0,2,1:T(4,128)S(1)} %fusion.38), channel_id=1, replica_groups=mesh['res'=16,'samp'=8] {'res'}, use_global_device_ids=true, to_apply=%region_1.2 | all-reduce | flops 52 | bytes 416 | tf_op jit(solution)/shard_map/psum | solution.py:149
  65.3 457.8 %while.17 = (s32[]{:T(128)}, f32[]{:T(128)}, f32[4]{0:T(128)S(1)}, f32[6,4,4,3,128]{4,2,1,3,0:T(4,128)}, s32[6,4]{1,0:T(8,128)}, /*index=5*/s32[24,5]{1,0:T(8,12...) while((s32[]{:T(128)}, f32[]{:T(128)}, f32[4]{0:T(128)S(1)}, ...), condition=%wide.region_12.13_spmd.clone, body=%wide.region_8.12_spmd.clone.sunk | while | flops 282550656 | bytes 19244344 | solution.py:145
  70.7 3.3 select_multiply_fusion.2
  75.5 14.8 %fusion.211 = (f32[4,4,128]{2,1,0:T(4,128)S(1)}, f32[4]{0:T(128)S(1)}) fusion(f32[4,5,128,128]{3,2,1,0:T(8,128)S(1)} %get-tuple-element.381, f32[4,5,128,128]{3,2,1,0:T(8,128)S(1)} %get-tuple-element.382, f32[4,4,5,128]{3,2,1,0:T(8,128)S(1)} %copy.383, f32[4,4,128]{2,1,0:T(4,128)S(1)} %get-tuple-element.386, f32[4,4,5,128]{3,2,1,0:T(8,128)S(1)} %copy.385, ...), kind=kLoop, calls=%fused_computation.30.clone.1 | loop fusion | flops 62912508 | bytes 4087824 | tf_op jit(solution)/shard_map/while/body/eval_jaxpr/vmap()/reduce_sum | solution.py:99
  90.4 16.9 %fusion.213 = f32[4,4,1,128,1]{3,2,4,1,0:T(1,128)S(1)} fusion(f32[4,5,128,128]{3,2,1,0:T(8,128)S(1)} %get-tuple-element.381, f32[4,5,128,128]{3,2,1,0:T(8,128)S(1)} %get-tuple-element.382, f32[4,4,5,128]{3,2,1,0:T(8,128)S(1)} %copy.383, f32[4,4,128]{2,1,0:T(4,128)S(1)} %get-tuple-element.386, f32[4,4,5,128]{3,2,1,0:T(8,128)S(1)} %copy.385, ...), kind=kOutput, calls=%fused_computation.29.clone.1 | convolution fusion | flops 70778880 | bytes 2818048 | tf_op jit(solution)/shard_map/while/body/eval_jaxpr/vmap(skij,skj->si)/dot_general | solution.py:102
  107.3 16.9 %fusion.214 = f32[4,4,1,128,1]{3,2,4,1,0:T(1,128)S(1)} fusion(f32[4,5,128,128]{3,2,1,0:T(8,128)S(1)} %get-tuple-element.381, f32[4,5,128,128]{3,2,1,0:T(8,128)S(1)} %get-tuple-element.382, f32[4,4,5,128]{3,2,1,0:T(8,128)S(1)} %copy.383, f32[4,4,128]{2,1,0:T(4,128)S(1)} %get-tuple-element.386, f32[4,4,5,128]{3,2,1,0:T(8,128)S(1)} %copy.385, ...), kind=kOutput, calls=%fused_computation.27.clone.1 | convolution fusion | flops 70778880 | bytes 2818048 | tf_op jit(solution)/shard_map/while/body/eval_jaxpr/vmap(skij,skj->si)/dot_general | solution.py:102
  124.2 16.9 %fusion.215 = f32[4,4,1,128,1]{3,2,4,1,0:T(1,128)S(1)} fusion(f32[4,5,128,128]{3,2,1,0:T(8,128)S(1)} %get-tuple-element.381, f32[4,5,128,128]{3,2,1,0:T(8,128)S(1)} %get-tuple-element.382, f32[4,4,5,128]{3,2,1,0:T(8,128)S(1)} %copy.383, f32[4,4,128]{2,1,0:T(4,128)S(1)} %get-tuple-element.386, f32[4,4,5,128]{3,2,1,0:T(8,128)S(1)} %copy.385, ...), kind=kOutput, calls=%fused_computation.28.clone.1 | convolution fusion | flops 70778880 | bytes 2818048 | tf_op jit(solution)/shard_map/while/body/eval_jaxpr/vmap(skij,skj->si)/dot_general | solution.py:102
  147.0 3.3 select_multiply_fusion.2
  151.8 14.8 %fusion.211 = (f32[4,4,128]{2,1,0:T(4,128)S(1)}, f32[4]{0:T(128)S(1)}) fusion(f32[4,5,128,128]{3,2,1,0:T(8,128)S(1)} %get-tuple-element.381, f32[4,5,128,128]{3,2,1,0:T(8,128)S(1)} %get-tuple-element.382, f32[4,4,5,128]{3,2,1,0:T(8,128)S(1)} %copy.383, f32[4,4,128]{2,1,0:T(4,128)S(1)} %get-tuple-element.386, f32[4,4,5,128]{3,2,1,0:T(8,128)S(1)} %copy.385, ...), kind=kLoop, calls=%fused_computation.30.clone.1 | loop fusion | flops 62912508 | bytes 4087824 | tf_op jit(solution)/shard_map/while/body/eval_jaxpr/vmap()/reduce_sum | solution.py:99
  166.6 16.9 %fusion.213 = f32[4,4,1,128,1]{3,2,4,1,0:T(1,128)S(1)} fusion(f32[4,5,128,128]{3,2,1,0:T(8,128)S(1)} %get-tuple-element.381, f32[4,5,128,128]{3,2,1,0:T(8,128)S(1)} %get-tuple-element.382, f32[4,4,5,128]{3,2,1,0:T(8,128)S(1)} %copy.383, f32[4,4,128]{2,1,0:T(4,128)S(1)} %get-tuple-element.386, f32[4,4,5,128]{3,2,1,0:T(8,128)S(1)} %copy.385, ...), kind=kOutput, calls=%fused_computation.29.clone.1 | convolution fusion | flops 70778880 | bytes 2818048 | tf_op jit(solution)/shard_map/while/body/eval_jaxpr/vmap(skij,skj->si)/dot_general | solution.py:102
  183.5 16.9 %fusion.214 = f32[4,4,1,128,1]{3,2,4,1,0:T(1,128)S(1)} fusion(f32[4,5,128,128]{3,2,1,0:T(8,128)S(1)} %get-tuple-element.381, f32[4,5,128,128]{3,2,1,0:T(8,128)S(1)} %get-tuple-element.382, f32[4,4,5,128]{3,2,1,0:T(8,128)S(1)} %copy.383, f32[4,4,128]{2,1,0:T(4,128)S(1)} %get-tuple-element.386, f32[4,4,5,128]{3,2,1,0:T(8,128)S(1)} %copy.385, ...), kind=kOutput, calls=%fused_computation.27.clone.1 | convolution fusion | flops 70778880 | bytes 2818048 | tf_op jit(solution)/shard_map/while/body/eval_jaxpr/vmap(skij,skj->si)/dot_general | solution.py:102
  200.4 16.9 %fusion.215 = f32[4,4,1,128,1]{3,2,4,1,0:T(1,128)S(1)} fusion(f32[4,5,128,128]{3,2,1,0:T(8,128)S(1)} %get-tuple-element.381, f32[4,5,128,128]{3,2,1,0:T(8,128)S(1)} %get-tuple-element.382, f32[4,4,5,128]{3,2,1,0:T(8,128)S(1)} %copy.383, f32[4,4,128]{2,1,0:T(4,128)S(1)} %get-tuple-element.386, f32[4,4,5,128]{3,2,1,0:T(8,128)S(1)} %copy.385, ...), kind=kOutput, calls=%fused_computation.28.clone.1 | convolution fusion | flops 70778880 | bytes 2818048 | tf_op jit(solution)/shard_map/while/body/eval_jaxpr/vmap(skij,skj->si)/dot_general | solution.py:102
  223.2 3.3 select_multiply_fusion.2
  228.1 14.8 %fusion.211 = (f32[4,4,128]{2,1,0:T(4,128)S(1)}, f32[4]{0:T(128)S(1)}) fusion(f32[4,5,128,128]{3,2,1,0:T(8,128)S(1)} %get-tuple-element.381, f32[4,5,128,128]{3,2,1,0:T(8,128)S(1)} %get-tuple-element.382, f32[4,4,5,128]{3,2,1,0:T(8,128)S(1)} %copy.383, f32[4,4,128]{2,1,0:T(4,128)S(1)} %get-tuple-element.386, f32[4,4,5,128]{3,2,1,0:T(8,128)S(1)} %copy.385, ...), kind=kLoop, calls=%fused_computation.30.clone.1 | loop fusion | flops 62912508 | bytes 4087824 | tf_op jit(solution)/shard_map/while/body/eval_jaxpr/vmap()/reduce_sum | solution.py:99
  242.9 16.9 %fusion.213 = f32[4,4,1,128,1]{3,2,4,1,0:T(1,128)S(1)} fusion(f32[4,5,128,128]{3,2,1,0:T(8,128)S(1)} %get-tuple-element.381, f32[4,5,128,128]{3,2,1,0:T(8,128)S(1)} %get-tuple-element.382, f32[4,4,5,128]{3,2,1,0:T(8,128)S(1)} %copy.383, f32[4,4,128]{2,1,0:T(4,128)S(1)} %get-tuple-element.386, f32[4,4,5,128]{3,2,1,0:T(8,128)S(1)} %copy.385, ...), kind=kOutput, calls=%fused_computation.29.clone.1 | convolution fusion | flops 70778880 | bytes 2818048 | tf_op jit(solution)/shard_map/while/body/eval_jaxpr/vmap(skij,skj->si)/dot_general | solution.py:102
  259.8 16.9 %fusion.214 = f32[4,4,1,128,1]{3,2,4,1,0:T(1,128)S(1)} fusion(f32[4,5,128,128]{3,2,1,0:T(8,128)S(1)} %get-tuple-element.381, f32[4,5,128,128]{3,2,1,0:T(8,128)S(1)} %get-tuple-element.382, f32[4,4,5,128]{3,2,1,0:T(8,128)S(1)} %copy.383, f32[4,4,128]{2,1,0:T(4,128)S(1)} %get-tuple-element.386, f32[4,4,5,128]{3,2,1,0:T(8,128)S(1)} %copy.385, ...), kind=kOutput, calls=%fused_computation.27.clone.1 | convolution fusion | flops 70778880 | bytes 2818048 | tf_op jit(solution)/shard_map/while/body/eval_jaxpr/vmap(skij,skj->si)/dot_general | solution.py:102
  276.7 16.9 %fusion.215 = f32[4,4,1,128,1]{3,2,4,1,0:T(1,128)S(1)} fusion(f32[4,5,128,128]{3,2,1,0:T(8,128)S(1)} %get-tuple-element.381, f32[4,5,128,128]{3,2,1,0:T(8,128)S(1)} %get-tuple-element.382, f32[4,4,5,128]{3,2,1,0:T(8,128)S(1)} %copy.383, f32[4,4,128]{2,1,0:T(4,128)S(1)} %get-tuple-element.386, f32[4,4,5,128]{3,2,1,0:T(8,128)S(1)} %copy.385, ...), kind=kOutput, calls=%fused_computation.28.clone.1 | convolution fusion | flops 70778880 | bytes 2818048 | tf_op jit(solution)/shard_map/while/body/eval_jaxpr/vmap(skij,skj->si)/dot_general | solution.py:102
  304.3 14.8 %fusion.211 = (f32[4,4,128]{2,1,0:T(4,128)S(1)}, f32[4]{0:T(128)S(1)}) fusion(f32[4,5,128,128]{3,2,1,0:T(8,128)S(1)} %get-tuple-element.381, f32[4,5,128,128]{3,2,1,0:T(8,128)S(1)} %get-tuple-element.382, f32[4,4,5,128]{3,2,1,0:T(8,128)S(1)} %copy.383, f32[4,4,128]{2,1,0:T(4,128)S(1)} %get-tuple-element.386, f32[4,4,5,128]{3,2,1,0:T(8,128)S(1)} %copy.385, ...), kind=kLoop, calls=%fused_computation.30.clone.1 | loop fusion | flops 62912508 | bytes 4087824 | tf_op jit(solution)/shard_map/while/body/eval_jaxpr/vmap()/reduce_sum | solution.py:99
  319.2 16.9 %fusion.213 = f32[4,4,1,128,1]{3,2,4,1,0:T(1,128)S(1)} fusion(f32[4,5,128,128]{3,2,1,0:T(8,128)S(1)} %get-tuple-element.381, f32[4,5,128,128]{3,2,1,0:T(8,128)S(1)} %get-tuple-element.382, f32[4,4,5,128]{3,2,1,0:T(8,128)S(1)} %copy.383, f32[4,4,128]{2,1,0:T(4,128)S(1)} %get-tuple-element.386, f32[4,4,5,128]{3,2,1,0:T(8,128)S(1)} %copy.385, ...), kind=kOutput, calls=%fused_computation.29.clone.1 | convolution fusion | flops 70778880 | bytes 2818048 | tf_op jit(solution)/shard_map/while/body/eval_jaxpr/vmap(skij,skj->si)/dot_general | solution.py:102
  336.1 16.9 %fusion.214 = f32[4,4,1,128,1]{3,2,4,1,0:T(1,128)S(1)} fusion(f32[4,5,128,128]{3,2,1,0:T(8,128)S(1)} %get-tuple-element.381, f32[4,5,128,128]{3,2,1,0:T(8,128)S(1)} %get-tuple-element.382, f32[4,4,5,128]{3,2,1,0:T(8,128)S(1)} %copy.383, f32[4,4,128]{2,1,0:T(4,128)S(1)} %get-tuple-element.386, f32[4,4,5,128]{3,2,1,0:T(8,128)S(1)} %copy.385, ...), kind=kOutput, calls=%fused_computation.27.clone.1 | convolution fusion | flops 70778880 | bytes 2818048 | tf_op jit(solution)/shard_map/while/body/eval_jaxpr/vmap(skij,skj->si)/dot_general | solution.py:102
  352.9 16.9 %fusion.215 = f32[4,4,1,128,1]{3,2,4,1,0:T(1,128)S(1)} fusion(f32[4,5,128,128]{3,2,1,0:T(8,128)S(1)} %get-tuple-element.381, f32[4,5,128,128]{3,2,1,0:T(8,128)S(1)} %get-tuple-element.382, f32[4,4,5,128]{3,2,1,0:T(8,128)S(1)} %copy.383, f32[4,4,128]{2,1,0:T(4,128)S(1)} %get-tuple-element.386, f32[4,4,5,128]{3,2,1,0:T(8,128)S(1)} %copy.385, ...), kind=kOutput, calls=%fused_computation.28.clone.1 | convolution fusion | flops 70778880 | bytes 2818048 | tf_op jit(solution)/shard_map/while/body/eval_jaxpr/vmap(skij,skj->si)/dot_general | solution.py:102
  380.6 14.8 %fusion.211 = (f32[4,4,128]{2,1,0:T(4,128)S(1)}, f32[4]{0:T(128)S(1)}) fusion(f32[4,5,128,128]{3,2,1,0:T(8,128)S(1)} %get-tuple-element.381, f32[4,5,128,128]{3,2,1,0:T(8,128)S(1)} %get-tuple-element.382, f32[4,4,5,128]{3,2,1,0:T(8,128)S(1)} %copy.383, f32[4,4,128]{2,1,0:T(4,128)S(1)} %get-tuple-element.386, f32[4,4,5,128]{3,2,1,0:T(8,128)S(1)} %copy.385, ...), kind=kLoop, calls=%fused_computation.30.clone.1 | loop fusion | flops 62912508 | bytes 4087824 | tf_op jit(solution)/shard_map/while/body/eval_jaxpr/vmap()/reduce_sum | solution.py:99
  395.4 16.9 %fusion.213 = f32[4,4,1,128,1]{3,2,4,1,0:T(1,128)S(1)} fusion(f32[4,5,128,128]{3,2,1,0:T(8,128)S(1)} %get-tuple-element.381, f32[4,5,128,128]{3,2,1,0:T(8,128)S(1)} %get-tuple-element.382, f32[4,4,5,128]{3,2,1,0:T(8,128)S(1)} %copy.383, f32[4,4,128]{2,1,0:T(4,128)S(1)} %get-tuple-element.386, f32[4,4,5,128]{3,2,1,0:T(8,128)S(1)} %copy.385, ...), kind=kOutput, calls=%fused_computation.29.clone.1 | convolution fusion | flops 70778880 | bytes 2818048 | tf_op jit(solution)/shard_map/while/body/eval_jaxpr/vmap(skij,skj->si)/dot_general | solution.py:102
  412.3 16.9 %fusion.214 = f32[4,4,1,128,1]{3,2,4,1,0:T(1,128)S(1)} fusion(f32[4,5,128,128]{3,2,1,0:T(8,128)S(1)} %get-tuple-element.381, f32[4,5,128,128]{3,2,1,0:T(8,128)S(1)} %get-tuple-element.382, f32[4,4,5,128]{3,2,1,0:T(8,128)S(1)} %copy.383, f32[4,4,128]{2,1,0:T(4,128)S(1)} %get-tuple-element.386, f32[4,4,5,128]{3,2,1,0:T(8,128)S(1)} %copy.385, ...), kind=kOutput, calls=%fused_computation.27.clone.1 | convolution fusion | flops 70778880 | bytes 2818048 | tf_op jit(solution)/shard_map/while/body/eval_jaxpr/vmap(skij,skj->si)/dot_general | solution.py:102
  429.2 16.9 %fusion.215 = f32[4,4,1,128,1]{3,2,4,1,0:T(1,128)S(1)} fusion(f32[4,5,128,128]{3,2,1,0:T(8,128)S(1)} %get-tuple-element.381, f32[4,5,128,128]{3,2,1,0:T(8,128)S(1)} %get-tuple-element.382, f32[4,4,5,128]{3,2,1,0:T(8,128)S(1)} %copy.383, f32[4,4,128]{2,1,0:T(4,128)S(1)} %get-tuple-element.386, f32[4,4,5,128]{3,2,1,0:T(8,128)S(1)} %copy.385, ...), kind=kOutput, calls=%fused_computation.28.clone.1 | convolution fusion | flops 70778880 | bytes 2818048 | tf_op jit(solution)/shard_map/while/body/eval_jaxpr/vmap(skij,skj->si)/dot_general | solution.py:102
  456.8 14.8 %fusion.211 = (f32[4,4,128]{2,1,0:T(4,128)S(1)}, f32[4]{0:T(128)S(1)}) fusion(f32[4,5,128,128]{3,2,1,0:T(8,128)S(1)} %get-tuple-element.381, f32[4,5,128,128]{3,2,1,0:T(8,128)S(1)} %get-tuple-element.382, f32[4,4,5,128]{3,2,1,0:T(8,128)S(1)} %copy.383, f32[4,4,128]{2,1,0:T(4,128)S(1)} %get-tuple-element.386, f32[4,4,5,128]{3,2,1,0:T(8,128)S(1)} %copy.385, ...), kind=kLoop, calls=%fused_computation.30.clone.1 | loop fusion | flops 62912508 | bytes 4087824 | tf_op jit(solution)/shard_map/while/body/eval_jaxpr/vmap()/reduce_sum | solution.py:99
  471.7 16.9 %fusion.213 = f32[4,4,1,128,1]{3,2,4,1,0:T(1,128)S(1)} fusion(f32[4,5,128,128]{3,2,1,0:T(8,128)S(1)} %get-tuple-element.381, f32[4,5,128,128]{3,2,1,0:T(8,128)S(1)} %get-tuple-element.382, f32[4,4,5,128]{3,2,1,0:T(8,128)S(1)} %copy.383, f32[4,4,128]{2,1,0:T(4,128)S(1)} %get-tuple-element.386, f32[4,4,5,128]{3,2,1,0:T(8,128)S(1)} %copy.385, ...), kind=kOutput, calls=%fused_computation.29.clone.1 | convolution fusion | flops 70778880 | bytes 2818048 | tf_op jit(solution)/shard_map/while/body/eval_jaxpr/vmap(skij,skj->si)/dot_general | solution.py:102
  488.6 16.9 %fusion.214 = f32[4,4,1,128,1]{3,2,4,1,0:T(1,128)S(1)} fusion(f32[4,5,128,128]{3,2,1,0:T(8,128)S(1)} %get-tuple-element.381, f32[4,5,128,128]{3,2,1,0:T(8,128)S(1)} %get-tuple-element.382, f32[4,4,5,128]{3,2,1,0:T(8,128)S(1)} %copy.383, f32[4,4,128]{2,1,0:T(4,128)S(1)} %get-tuple-element.386, f32[4,4,5,128]{3,2,1,0:T(8,128)S(1)} %copy.385, ...), kind=kOutput, calls=%fused_computation.27.clone.1 | convolution fusion | flops 70778880 | bytes 2818048 | tf_op jit(solution)/shard_map/while/body/eval_jaxpr/vmap(skij,skj->si)/dot_general | solution.py:102
  505.5 16.9 %fusion.215 = f32[4,4,1,128,1]{3,2,4,1,0:T(1,128)S(1)} fusion(f32[4,5,128,128]{3,2,1,0:T(8,128)S(1)} %get-tuple-element.381, f32[4,5,128,128]{3,2,1,0:T(8,128)S(1)} %get-tuple-element.382, f32[4,4,5,128]{3,2,1,0:T(8,128)S(1)} %copy.383, f32[4,4,128]{2,1,0:T(4,128)S(1)} %get-tuple-element.386, f32[4,4,5,128]{3,2,1,0:T(8,128)S(1)} %copy.385, ...), kind=kOutput, calls=%fused_computation.28.clone.1 | convolution fusion | flops 70778880 | bytes 2818048 | tf_op jit(solution)/shard_map/while/body/eval_jaxpr/vmap(skij,skj->si)/dot_general | solution.py:102
  523.0 29.7 %all-reduce = (f32[4]{0:T(128)S(1)}, f32[4]{0:T(128)S(1)}, f32[]{:T(128)}) all-reduce(f32[4]{0:T(128)S(1)} %get-tuple-element.121, f32[4]{0:T(128)} %get-tuple-element.267, f32[]{:T(128)} %get-tuple-element.122), channel_id=1, replica_groups=mesh['res'=16,'samp'=8] {'res'}, use_global_device_ids=true, to_apply=%region_13.14 | all-reduce | flops 9 | bytes 72 | tf_op jit(solution)/shard_map/psum | solution.py:154
  555.2 27.9 %psum.63 = f32[]{:T(128)} all-reduce(f32[]{:T(128)} %get-tuple-element.228), channel_id=1, replica_groups=mesh['res'=16,'samp'=8] {'samp'}, use_global_device_ids=true, to_apply=%region_16.17 | all-reduce | flops 1 | bytes 8 | tf_op jit(solution)/shard_map/psum | solution.py:160
  (392 shorter events, 79.9 us)
Async XLA Ops:
  0.6 10.8 %copy-start.4 = (f32[4,3,3072]{2,0,1:T(4,128)S(1)}, f32[4,3,3072]{2,0,1:T(4,128)}, u32[]{:S(2)}) copy-start(f32[4,3,3072]{2,0,1:T(4,128)} %param.7) | copy-start | bytes 442372
  0.6 10.1 %copy-start.3 = (f32[3,3072]{1,0:T(4,128)S(1)}, f32[3,3072]{1,0:T(4,128)}, u32[]{:S(2)}) copy-start(f32[3,3072]{1,0:T(4,128)} %param.8) | copy-start | bytes 110596
  0.7 10.0 %copy-start.6 = (s32[24,5]{0,1:T(8,128)S(1)}, s32[24,5]{0,1:T(8,128)}, u32[]{:S(2)}) copy-start(s32[24,5]{0,1:T(8,128)} %param.10) | copy-start | bytes 1444
  4.0 61.2 %collective-permute-start.1 = (f32[16,3072]{1,0:T(8,128)S(1)}, f32[16,3072]{1,0:T(8,128)S(1)}, u32[]{:S(2)}, u32[]{:S(2)}) collective-permute-start(f32[16,3072]{1,0:T(8,128)S(1)} %pad_maximum_fusion.1), channel_id=1, source_target_pairs={{8,0},{16,8},{24,16},{32,24},{40,32},{48,40},{56,48},{64,56},{72,6... | collective-permute-start | bytes 589832 | tf_op jit(solution)/shard_map/ppermute | solution.py:21
  5.3 59.9 %collective-permute-start = (f32[16,3072]{1,0:T(8,128)S(1)}, f32[16,3072]{1,0:T(8,128)S(1)}, u32[]{:S(2)}, u32[]{:S(2)}) collective-permute-start(f32[16,3072]{1,0:T(8,128)S(1)} %pad_maximum_fusion.1), channel_id=1, source_target_pairs={{0,8},{8,16},{16,24},{24,32},{32,40},{40,48},{48,56},{56,64},{64,7... | collective-permute-start | bytes 589832 | tf_op jit(solution)/shard_map/ppermute | solution.py:18
  11.4 50.1 %copy-start.7 = (f32[4]{0:T(128)S(1)}, f32[4]{0:T(128)}, u32[]{:S(2)}) copy-start(f32[4]{0:T(128)} %param.11) | copy-start | bytes 52
  75.5 14.8 %copy-start.2 = (f32[4,4,5,128,1]{3,0,2,1,4:T(4,128)S(1)}, f32[4,4,5,128,1]{3,0,2,1,4:T(4,128)}, u32[]{:S(2)}) copy-start(f32[4,4,5,128,1]{3,0,2,1,4:T(4,128)} %get-tuple-element.393) | copy-start | bytes 122884 | tf_op jit(solution)/shard_map/while
  90.4 16.9 %copy-start.1 = (f32[4,4,5,128,1]{3,0,2,1,4:T(4,128)S(1)}, f32[4,4,5,128,1]{3,0,2,1,4:T(4,128)}, u32[]{:S(2)}) copy-start(f32[4,4,5,128,1]{3,0,2,1,4:T(4,128)} %get-tuple-element.395) | copy-start | bytes 122884 | tf_op jit(solution)/shard_map/while
  107.3 16.9 %copy-start = (f32[4,4,5,128,1]{3,0,2,1,4:T(4,128)S(1)}, f32[4,4,5,128,1]{3,0,2,1,4:T(4,128)}, u32[]{:S(2)}) copy-start(f32[4,4,5,128,1]{3,0,2,1,4:T(4,128)} %get-tuple-element.396) | copy-start | bytes 122884 | tf_op jit(solution)/shard_map/while
  151.8 14.8 %copy-start.2 = (f32[4,4,5,128,1]{3,0,2,1,4:T(4,128)S(1)}, f32[4,4,5,128,1]{3,0,2,1,4:T(4,128)}, u32[]{:S(2)}) copy-start(f32[4,4,5,128,1]{3,0,2,1,4:T(4,128)} %get-tuple-element.393) | copy-start | bytes 122884 | tf_op jit(solution)/shard_map/while
  166.6 16.9 %copy-start.1 = (f32[4,4,5,128,1]{3,0,2,1,4:T(4,128)S(1)}, f32[4,4,5,128,1]{3,0,2,1,4:T(4,128)}, u32[]{:S(2)}) copy-start(f32[4,4,5,128,1]{3,0,2,1,4:T(4,128)} %get-tuple-element.395) | copy-start | bytes 122884 | tf_op jit(solution)/shard_map/while
  183.5 16.9 %copy-start = (f32[4,4,5,128,1]{3,0,2,1,4:T(4,128)S(1)}, f32[4,4,5,128,1]{3,0,2,1,4:T(4,128)}, u32[]{:S(2)}) copy-start(f32[4,4,5,128,1]{3,0,2,1,4:T(4,128)} %get-tuple-element.396) | copy-start | bytes 122884 | tf_op jit(solution)/shard_map/while
  228.0 14.8 %copy-start.2 = (f32[4,4,5,128,1]{3,0,2,1,4:T(4,128)S(1)}, f32[4,4,5,128,1]{3,0,2,1,4:T(4,128)}, u32[]{:S(2)}) copy-start(f32[4,4,5,128,1]{3,0,2,1,4:T(4,128)} %get-tuple-element.393) | copy-start | bytes 122884 | tf_op jit(solution)/shard_map/while
  242.9 16.9 %copy-start.1 = (f32[4,4,5,128,1]{3,0,2,1,4:T(4,128)S(1)}, f32[4,4,5,128,1]{3,0,2,1,4:T(4,128)}, u32[]{:S(2)}) copy-start(f32[4,4,5,128,1]{3,0,2,1,4:T(4,128)} %get-tuple-element.395) | copy-start | bytes 122884 | tf_op jit(solution)/shard_map/while
  259.8 16.9 %copy-start = (f32[4,4,5,128,1]{3,0,2,1,4:T(4,128)S(1)}, f32[4,4,5,128,1]{3,0,2,1,4:T(4,128)}, u32[]{:S(2)}) copy-start(f32[4,4,5,128,1]{3,0,2,1,4:T(4,128)} %get-tuple-element.396) | copy-start | bytes 122884 | tf_op jit(solution)/shard_map/while
  304.3 14.8 %copy-start.2 = (f32[4,4,5,128,1]{3,0,2,1,4:T(4,128)S(1)}, f32[4,4,5,128,1]{3,0,2,1,4:T(4,128)}, u32[]{:S(2)}) copy-start(f32[4,4,5,128,1]{3,0,2,1,4:T(4,128)} %get-tuple-element.393) | copy-start | bytes 122884 | tf_op jit(solution)/shard_map/while
  319.1 16.9 %copy-start.1 = (f32[4,4,5,128,1]{3,0,2,1,4:T(4,128)S(1)}, f32[4,4,5,128,1]{3,0,2,1,4:T(4,128)}, u32[]{:S(2)}) copy-start(f32[4,4,5,128,1]{3,0,2,1,4:T(4,128)} %get-tuple-element.395) | copy-start | bytes 122884 | tf_op jit(solution)/shard_map/while
  336.0 16.9 %copy-start = (f32[4,4,5,128,1]{3,0,2,1,4:T(4,128)S(1)}, f32[4,4,5,128,1]{3,0,2,1,4:T(4,128)}, u32[]{:S(2)}) copy-start(f32[4,4,5,128,1]{3,0,2,1,4:T(4,128)} %get-tuple-element.396) | copy-start | bytes 122884 | tf_op jit(solution)/shard_map/while
  380.6 14.8 %copy-start.2 = (f32[4,4,5,128,1]{3,0,2,1,4:T(4,128)S(1)}, f32[4,4,5,128,1]{3,0,2,1,4:T(4,128)}, u32[]{:S(2)}) copy-start(f32[4,4,5,128,1]{3,0,2,1,4:T(4,128)} %get-tuple-element.393) | copy-start | bytes 122884 | tf_op jit(solution)/shard_map/while
  395.4 16.9 %copy-start.1 = (f32[4,4,5,128,1]{3,0,2,1,4:T(4,128)S(1)}, f32[4,4,5,128,1]{3,0,2,1,4:T(4,128)}, u32[]{:S(2)}) copy-start(f32[4,4,5,128,1]{3,0,2,1,4:T(4,128)} %get-tuple-element.395) | copy-start | bytes 122884 | tf_op jit(solution)/shard_map/while
  412.3 16.9 %copy-start = (f32[4,4,5,128,1]{3,0,2,1,4:T(4,128)S(1)}, f32[4,4,5,128,1]{3,0,2,1,4:T(4,128)}, u32[]{:S(2)}) copy-start(f32[4,4,5,128,1]{3,0,2,1,4:T(4,128)} %get-tuple-element.396) | copy-start | bytes 122884 | tf_op jit(solution)/shard_map/while
  456.8 14.8 %copy-start.2 = (f32[4,4,5,128,1]{3,0,2,1,4:T(4,128)S(1)}, f32[4,4,5,128,1]{3,0,2,1,4:T(4,128)}, u32[]{:S(2)}) copy-start(f32[4,4,5,128,1]{3,0,2,1,4:T(4,128)} %get-tuple-element.393) | copy-start | bytes 122884 | tf_op jit(solution)/shard_map/while
  471.7 16.9 %copy-start.1 = (f32[4,4,5,128,1]{3,0,2,1,4:T(4,128)S(1)}, f32[4,4,5,128,1]{3,0,2,1,4:T(4,128)}, u32[]{:S(2)}) copy-start(f32[4,4,5,128,1]{3,0,2,1,4:T(4,128)} %get-tuple-element.395) | copy-start | bytes 122884 | tf_op jit(solution)/shard_map/while
  488.6 16.9 %copy-start = (f32[4,4,5,128,1]{3,0,2,1,4:T(4,128)S(1)}, f32[4,4,5,128,1]{3,0,2,1,4:T(4,128)}, u32[]{:S(2)}) copy-start(f32[4,4,5,128,1]{3,0,2,1,4:T(4,128)} %get-tuple-element.396) | copy-start | bytes 122884 | tf_op jit(solution)/shard_map/while
  523.0 62.5 %copy-start.5 = (f32[4,3,3072]{2,0,1:T(4,128)S(1)}, f32[4,3,3072]{2,0,1:T(4,128)}, u32[]{:S(2)}) copy-start(f32[4,3,3072]{2,0,1:T(4,128)} %get-tuple-element.268) | copy-start | bytes 442372
where the time goes:
time: 589 us; the launch traced here: 588 us
  matrix products  315 us (53%)
  other arithmetic  139 us (24%)
  blocking collectives  92.3 us (16%)
  local copies, waits for them, and re-layouts  28 us (5%)
    dot_general x18, matrix products, pair_terms(): jnp.einsum('skij,skj->si', factor, far_pred[:, component], precision=prec...  304 us
    reduce_sum x6, other arithmetic, pair_terms(): weight_row = jnp.sum(factor, axis=(1, 3))  88.8 us
    psum x1, blocking collectives, shards(): lax.psum((weight_sum, pred_sum, true_sum, cross), 'res')  34.7 us
    psum x1, blocking collectives, shards(): lax.psum((square_local, score_local, pair_local), 'res')  29.7 us
    psum x1, blocking collectives, shards(): copy_sum = lax.psum(jnp.sum(copy_loss), 'samp')  27.9 us
    mul x6, other arithmetic, pair_terms(): score_sum = jnp.sum(mask_fwd * pair_score, axis=(1, 2, 3))  19.9 us
  transfers between devices with their start and end apart: 2, of which 0 were waited for; matrix products, arithmetic and copies ran while one was open for 3% of the time, Pallas kernels for 0%

commit v1 on v0

v1 whole, which is shorter than its diff:
```python
import functools

import jax
import jax.numpy as jnp
from jax import lax
from jax.experimental import pallas as pl
from jax.experimental.pallas import tpu as pltpu
from jax.sharding import PartitionSpec as P

F32, BF16 = jnp.float32, jnp.bfloat16
MESH = pl.DeviceIdType.MESH
TILE = 128
BAND = 2
CHUNK = 16
PARTS = 16
LEVELS = (0.25, 0.5, 1.0, 2.0)
STEEP = 1e15
SIGMA = 16.0
VMEM_BYTES = 56 * 1024 * 1024


def lanes(tile, count=1):
    return pl.ds(pl.multiple_of(tile * TILE, TILE), count * TILE)


def atom_weight(kind):
    return jnp.where(kind == 1, 5.0, jnp.where(kind == 2, 10.0, 1.0)).astype(F32)


def pieces(x):
    high = x.astype(BF16).astype(F32)
    mid = (x - high).astype(BF16).astype(F32)
    return high, mid, (x - high) - mid


def fill_rows(rows, split, moved, at, pred, true, kind):
    copies, _, width = pred.shape
    span = pl.ds(at, width)
    for s in range(copies):
        half = 0.5 * pred[s]
        rows[3 * s : 3 * s + 3, span] = half
        unit = jnp.concatenate([jnp.ones((1, width), F32), jnp.zeros((4, width), F32)], axis=0)
        parts = pieces(jnp.concatenate([half, unit], axis=0))
        stack = jnp.concatenate([*parts, jnp.zeros((8, width), F32)], axis=0)
        moved[s, :, span] = stack.astype(BF16)
    rows[3 * copies : 3 * copies + 3, span] = 0.5 * true[...]
    rows[3 * copies + 3 : 3 * copies + 4, span] = jnp.where(kind[...] == 1, 15.0, 7.5).astype(F32)
    if split is not None:
        high, mid, low = pieces(rows[:, span])
        split[0:PARTS, span] = high
        split[PARTS : 2 * PARTS, span] = mid
        split[2 * PARTS : 3 * PARTS, span] = low


def fill_select(select):
    row = lax.broadcasted_iota(jnp.int32, select.shape, 0) % PARTS
    column = lax.broadcasted_iota(jnp.int32, select.shape, 1) // TILE
    select[...] = jnp.where(row == column, 1.0, 0.0).astype(BF16)


def spread_steps(split, select, wide, slot, tile):
    turned = jnp.transpose(split[:, lanes(tile)]).astype(BF16)

    def step(k):
        part = slice(2 * k * TILE, 2 * (k + 1) * TILE)
        wide[slot, :, part] = jnp.dot(turned, select[:, part], preferred_element_type=F32)

    return [functools.partial(step, k) for k in range(PARTS // 2)]


def masks(rows, near, wide, slot, dist, mask, flag=None, own=False):
    copies = (PARTS - 4) // 3
    true = [rows[3 * copies + c : 3 * copies + c + 1, near] for c in range(3)]
    cut = rows[3 * copies + 3 : 3 * copies + 4, near]
    count = jnp.zeros((8, TILE), F32)

    def wide_row(r, band):
        return wide[slot, band, r * TILE : (r + 1) * TILE]

    for start in range(0, TILE, CHUNK):
        band = slice(start, start + CHUNK)
        gap = [wide_row(3 * copies + c, band) - true[c] for c in range(3)]
        square = gap[0] * gap[0] + gap[1] * gap[1] + (gap[2] * gap[2] + 2.5e-7)
        length = square * lax.rsqrt(square)
        both = jnp.where(length < cut, 1.0, 0.0) + jnp.where(
            length < wide_row(3 * copies + 3, band), 1.0, 0.0
        )
        if own:
            row = lax.broadcasted_iota(jnp.int32, (CHUNK, TILE), 0) + start
            both = jnp.where(row == lax.broadcasted_iota(jnp.int32, (CHUNK, TILE), 1), 0.0, both)
        if flag is not None:
            both = both * flag
        dist[band] = length
        mask[band] = both
        for v in range(0, CHUNK, 8):
            count += both[v : v + 8]
    return count


def forces(rows, near, s, wide, slot, dist, mask, force, fillers):
    mate = [rows[3 * s + c : 3 * s + c + 1, near] for c in range(3)]
    total = jnp.zeros((8, TILE), F32)
    for start in range(0, TILE, CHUNK):
        band = slice(start, start + CHUNK)
        gap = [
            wide[slot, band, (3 * s + c) * TILE : (3 * s + c + 1) * TILE] - mate[c] for c in range(3)
        ]
        square = gap[0] * gap[0] + gap[1] * gap[1] + (gap[2] * gap[2] + 2.5e-7)
        inverse = lax.rsqrt(square)
        excess = square * inverse - dist[band]
        spread = jnp.abs(excess)
        th = [jnp.tanh(level - spread) for level in LEVELS]
        both = mask[band]
        score = both * ((th[0] + th[1]) + (th[2] + th[3]))
        for v in range(0, CHUNK, 8):
            total += score[v : v + 8]
        slope = 4.0 - ((th[0] * th[0] + th[1] * th[1]) + (th[2] * th[2] + th[3] * th[3]))
        pull = ((both * inverse) * jnp.tanh(excess * STEEP)) * slope
        high = pull.astype(BF16)
        force[s, band, 0:TILE] = high
        force[s, band, TILE : 2 * TILE] = (pull - high.astype(F32)).astype(BF16)
        if fillers:
            fillers.pop(0)()
    return total


def fold(x):
    return (x[0:8] + x[8:16]) + x[16:24]


def down(moved, s, span, force):
    out = jnp.dot(moved[s, :, span], force[s], preferred_element_type=F32)
    return fold(out[:, 0:TILE] + out[:, TILE : 2 * TILE])


def across(moved, s, span, force):
    block = moved[s, :, span]
    return fold(
        lax.dot_general(
            jnp.concatenate([block, block], axis=1),
            force[s],
            (((1,), (1,)), ((), ())),
            preferred_element_type=F32,
        )
    )


def inner_kernel(
    pred, true, kind, partners, acc, sums, rows, split, moved, select, wide, dist, mask, force, pairs
):
    copies, _, atoms = pred.shape
    tiles = atoms // TILE
    first = lax.axis_index("res") * tiles

    def look(g, n):
        for k in range(1, partners.shape[1]):
            q = partners[g, k] - first
            pairs[n] = g
            pairs[n + 1] = q
            n = n + jnp.where((q > g) & (q < tiles), 2, 0)
        return n

    count = lax.fori_loop(0, tiles, look, 0)
    pairs[count] = 0
    fill_rows(rows, split, moved, 0, pred, true, kind)
    fill_select(select)
    acc[...] = jnp.zeros_like(acc)
    sums[...] = jnp.zeros_like(sums)
    for step in spread_steps(split, select, wide, 0, pairs[0]):
        step()

    def visit(p, carry):
        g, q, later = pairs[2 * p], pairs[2 * p + 1], pairs[2 * p + 2]
        slot = lax.rem(p, 2)
        near, span = lanes(q), lanes(g)
        fillers = []
        for step in spread_steps(split, select, wide, 1 - slot, later):
            fillers += [step, lambda: None, lambda: None]
        sums[0] += masks(rows, near, wide, slot, dist, mask)
        for s in range(copies):
            sums[1 + s] += forces(rows, near, s, wide, slot, dist, mask, force, fillers)
            acc[q, s] += down(moved, s, span, force)
            acc[g, s] += across(moved, s, near, force)
        return carry

    lax.fori_loop(0, count // 2, visit, 0)


def outer_kernel(
    res,
    samp,
    pred,
    true,
    kind,
    partners,
    noise,
    inner,
    inner_sums,
    copy_loss,
    mean_loss,
    grad,
    rows,
    moved,
    split,
    select,
    wide,
    dist,
    mask,
    force,
    acc,
    sums,
    halo_pred,
    halo_true,
    halo_kind,
    back,
    back_in,
    moment,
    moments,
    part,
    parts,
    loss,
    losses,
    turn,
    deviation,
    halo_send,
    halo_recv,
    back_send,
    back_recv,
    moment_send,
    moment_recv,
    part_send,
    part_recv,
    loss_send,
    loss_recv,
):
    copies, _, atoms = pred.shape
    tiles = atoms // TILE
    r, v = lax.axis_index("res"), lax.axis_index("samp")
    left, right = lax.rem(r + res - 1, res), lax.rem(r + 1, res)

    barrier = pltpu.get_barrier_semaphore()

    def greet_res(k, carry):
        pl.semaphore_signal(
            barrier, inc=1, device_id=(lax.rem(r + k, res), v), device_id_type=MESH
        )
        return carry

    def greet_samp(k, carry):
        pl.semaphore_signal(
            barrier, inc=1, device_id=(r, lax.rem(v + k, samp)), device_id_type=MESH
        )
        return carry

    lax.fori_loop(1, res, greet_res, 0)
    lax.fori_loop(1, samp, greet_samp, 0)

    fill_rows(rows, split, moved, 0, pred, true, kind)
    fill_select(select)
    weight = atom_weight(kind[...])
    lane = lax.broadcasted_iota(jnp.int32, (4, TILE), 1)
    for s in range(copies):
        block = jnp.concatenate([pred[s], jnp.ones((1, atoms), F32)], axis=0)
        packed = jnp.zeros((4, TILE), F32)
        for k in range(4):
            by = weight if k == 0 else weight * true[k - 1 : k, :]
            packed = jnp.where(lane == k, jnp.sum(block * by, axis=1, keepdims=True), packed)
        moment[4 * s : 4 * s + 4, :] = packed

    acc[...] = inner[...]
    sums[...] = jnp.zeros_like(sums)
    for step in spread_steps(split, select, wide, 0, 0):
        step()

    def visit_own(g, carry):
        slot = lax.rem(g, 2)
        near = lanes(g)
        fillers = []
        for step in spread_steps(split, select, wide, 1 - slot, lax.rem(g + 1, tiles)):
            fillers += [step, lambda: None, lambda: None]
        sums[0] += masks(rows, near, wide, slot, dist, mask, own=True)
        for s in range(copies):
            sums[1 + s] += forces(rows, near, s, wide, slot, dist, mask, force, fillers)
            acc[g, s] += down(moved, s, near, force)
        return carry

    early = tiles // 4
    lax.fori_loop(0, early, visit_own, 0)

    pl.semaphore_wait(barrier, res - 1 + samp - 1)

    edge = pl.ds(0, BAND * TILE)
    halo = [
        pltpu.make_async_remote_copy(
            src_ref=source,
            dst_ref=target,
            send_sem=halo_send.at[k],
            recv_sem=halo_recv.at[k],
            device_id=(left, v),
            device_id_type=MESH,
        )
        for k, (source, target) in enumerate(
            [
                (pred.at[:, :, edge], halo_pred),
                (true.at[:, edge], halo_true),
                (kind.at[:, edge], halo_kind),
            ]
        )
    ]
    for copy in halo:
        copy.start()

    def to_res(source, target, send, recv, k):
        peer = lax.rem(r + k, res)
        return pltpu.make_async_remote_copy(
            src_ref=source,
            dst_ref=target.at[r],
            send_sem=send.at[k],
            recv_sem=recv.at[r],
            device_id=(peer, v),
            device_id_type=MESH,
        )

    def from_res(source, target, send, recv, k):
        peer = lax.rem(r + k, res)
        return pltpu.make_async_remote_copy(
            src_ref=source,
            dst_ref=target.at[peer],
            send_sem=send.at[k],
            recv_sem=recv.at[peer],
            device_id=(peer, v),
            device_id_type=MESH,
        )

    def start_res(source, target, send, recv):
        def body(k, carry):
            to_res(source, target, send, recv, k).start()
            return carry

        lax.fori_loop(1, res, body, 0)

    def wait_res(source, target, send, recv):
        def body(k, carry):
            from_res(source, target, send, recv, k).wait_recv()
            to_res(source, target, send, recv, k).wait_send()
            return carry

        lax.fori_loop(1, res, body, 0)

    moments[r] = moment[...]
    start_res(moment, moments, moment_send, moment_recv)

    middle = tiles // 2
    lax.fori_loop(early, middle, visit_own, 0)

    for copy in halo:
        copy.wait()
    fill_rows(rows, None, moved, atoms, halo_pred, halo_true, halo_kind)
    back[...] = jnp.zeros_like(back)
    for i, j in ((tiles - 2, tiles), (tiles - 1, tiles), (tiles - 1, tiles + 1)):
        for step in spread_steps(split, select, wide, 0, i):
            step()
        near, span = slice(j * TILE, (j + 1) * TILE), slice(i * TILE, (i + 1) * TILE)
        listed = jnp.where(partners[i : i + 1, :] == r * tiles + j, 1.0, 0.0).astype(F32)
        flag = jnp.max(listed, axis=1, keepdims=True)
        sums[5] += masks(rows, near, wide, 0, dist, mask, flag=flag)
        for s in range(copies):
            sums[6 + s] += forces(rows, near, s, wide, 0, dist, mask, force, [])
            back[j - tiles, s] += down(moved, s, span, force)
            acc[i, s] += across(moved, s, near, force)
    returned = pltpu.make_async_remote_copy(
        src_ref=back,
        dst_ref=back_in,
        send_sem=back_send,
        recv_sem=back_recv,
        device_id=(right, v),
        device_id_type=MESH,
    )
    returned.start()
    for step in spread_steps(split, select, wide, middle % 2, middle):
        step()
    lax.fori_loop(middle, tiles, visit_own, 0)
    returned.wait()
    for t in range(BAND):
        acc[t] += back_in[t]

    wait_res(moment, moments, moment_send, moment_recv)
    total = moments[0]
    for k in range(1, res):
        total = total + moments[k]
    turn[0] = total

    def column(a, k):
        picked = turn[0, pl.ds(a, copies, stride=4), :]
        return jnp.broadcast_to(picked[:, k : k + 1], (copies, TILE))

    weight_sum = column(3, 0)
    true_mean = [column(3, 1 + d) / weight_sum for d in range(3)]
    pred_sum = [column(c, 0) for c in range(3)]
    cov = [[column(c, 1 + d) - pred_sum[c] * true_mean[d] for d in range(3)] for c in range(3)]
    square = sum(cov[c][d] * cov[c][d] for c in range(3) for d in range(3))
    frobenius = jnp.sqrt(square)
    polar = tuple(cov[c][d] / frobenius for c in range(3) for d in range(3))

    def sweep(_, flat):
        m = [flat[3 * c : 3 * c + 3] for c in range(3)]
        gram = {}
        for a in range(3):
            for c in range(a, 3):
                gram[a, c] = gram[c, a] = m[a][0] * m[c][0] + m[a][1] * m[c][1] + m[a][2] * m[c][2]
        return tuple(
            1.5 * m[a][d]
            - 0.5 * (gram[a, 0] * m[0][d] + gram[a, 1] * m[1][d] + gram[a, 2] * m[2][d])
            for a in range(3)
            for d in range(3)
        )

    polar = lax.fori_loop(0, 20, sweep, polar)
    for c in range(3):
        for d in range(3):
            turn[1 + d, pl.ds(c, copies, stride=4), :] = polar[3 * c + d]
        turn[4, pl.ds(c, copies, stride=4), :] = pred_sum[c] / weight_sum
        turn[5, pl.ds(c, copies, stride=4), :] = true_mean[c]
    zero = jnp.zeros((1, TILE), F32)
    part[4 + copies :, :] = jnp.zeros((16 - 4 - copies, TILE), F32)
    for s in range(copies):
        spin = [turn[1 + d, 4 * s : 4 * s + 3, :] for d in range(3)]
        mean = [turn[5, 4 * s + d : 4 * s + d + 1, :] for d in range(3)]
        offset = turn[4, 4 * s : 4 * s + 3, :]
        error = jnp.zeros((3, TILE), F32)
        for t in range(tiles):
            span = slice(t * TILE, (t + 1) * TILE)
            target = offset
            for d in range(3):
                target = target + spin[d] * (true[d : d + 1, span] - mean[d])
            away = pred[s, :, span] - target
            scaled = atom_weight(kind[:, span]) * away
            deviation[s, :, span] = scaled
            error = error + scaled * away
        count = 0.5 * sums[0] + sums[5] + inner_sums[0]
        score = 0.5 * count + 0.125 * (0.5 * sums[1 + s] + sums[6 + s] + inner_sums[1 + s])
        part[s : s + 1, :] = jnp.sum(score, axis=0, keepdims=True)
        part[4 + s : 5 + s, :] = jnp.sum(error, axis=0, keepdims=True)
        if s == 0:
            part[8:9, :] = jnp.sum(count, axis=0, keepdims=True)

    parts[r] = part[...]
    start_res(part, parts, part_send, part_recv)
    wait_res(part, parts, part_send, part_recv)
    total = parts[0]
    for k in range(1, res):
        total = total + parts[k]
    total = jnp.broadcast_to(jnp.sum(total, axis=1, keepdims=True), (16, TILE))
    pair_total = total[8:9]
    weight_all = weight_sum[0:1]
    own_loss = zero
    factor = []
    for s in range(copies):
        level = jnp.broadcast_to(noise[0:1, s : s + 1], (1, TILE))
        scale = (level * level + SIGMA * SIGMA) / (level * SIGMA * (level * SIGMA))
        factor.append(scale)
        this = scale * (total[4 + s : 5 + s] / (3.0 * weight_all)) + 1.0 - total[s : s + 1] / pair_total
        copy_loss[s] = this[0, 0]
        own_loss = own_loss + this
    loss[...] = jnp.broadcast_to(own_loss, loss.shape)
    losses[v] = loss[...]

    def to_samp(k):
        return pltpu.make_async_remote_copy(
            src_ref=loss,
            dst_ref=losses.at[v],
            send_sem=loss_send.at[k],
            recv_sem=loss_recv.at[v],
            device_id=(r, lax.rem(v + k, samp)),
            device_id_type=MESH,
        )

    def from_samp(k):
        peer = lax.rem(v + k, samp)
        return pltpu.make_async_remote_copy(
            src_ref=loss,
            dst_ref=losses.at[peer],
            send_sem=loss_send.at[k],
            recv_sem=loss_recv.at[peer],
            device_id=(r, peer),
            device_id_type=MESH,
        )

    def start_samp(k, carry):
        to_samp(k).start()
        return carry

    def wait_samp(k, carry):
        from_samp(k).wait_recv()
        to_samp(k).wait_send()
        return carry

    lax.fori_loop(1, samp, start_samp, 0)

    atom_total = float(atoms * res)
    pull_scale = atom_total / pair_total
    for s in range(copies):
        step_scale = (32.0 * atom_total) * factor[s] / (3.0 * weight_all)
        for t in range(tiles):
            span = slice(t * TILE, (t + 1) * TILE)
            near = acc[t, s]
            pull = (0.5 * pred[s, :, span]) * near[3:4] - near[0:3]
            grad[s, :, span] = step_scale * deviation[s, :, span] + pull_scale * pull

    lax.fori_loop(1, samp, wait_samp, 0)
    whole = losses[0]
    for k in range(1, samp):
        whole = whole + losses[k]
    mean_loss[0] = whole[0, 0] / float(copies * samp)


def shards(res, samp, coords_pred, coords_true, atom_kind, partners, noise_level):
    copies, _, atoms = coords_pred.shape
    tiles = atoms // TILE
    kind = atom_kind.reshape(1, atoms)
    vmem, smem = pl.BlockSpec(memory_space=pltpu.VMEM), pl.BlockSpec(memory_space=pltpu.SMEM)
    spread = [
        pltpu.VMEM((3 * PARTS, PARTS * TILE), BF16),
        pltpu.VMEM((2, TILE, PARTS * TILE), F32),
        pltpu.VMEM((TILE, TILE), F32),
        pltpu.VMEM((TILE, TILE), F32),
        pltpu.VMEM((copies, TILE, 2 * TILE), BF16),
    ]
    inner, inner_sums = pl.pallas_call(
        inner_kernel,
        name="inner_pairs",
        out_shape=(
            jax.ShapeDtypeStruct((tiles, copies, 8, TILE), F32),
            jax.ShapeDtypeStruct((1 + copies, 8, TILE), F32),
        ),
        in_specs=[vmem, vmem, vmem, smem],
        out_specs=(vmem, vmem),
        scratch_shapes=[
            pltpu.VMEM((PARTS, atoms), F32),
            pltpu.VMEM((3 * PARTS, atoms), F32),
            pltpu.VMEM((copies, 32, atoms), BF16),
            *spread,
            pltpu.SMEM((2 * tiles * BAND + 8,), jnp.int32),
        ],
        compiler_params=pltpu.CompilerParams(vmem_limit_bytes=VMEM_BYTES),
    )(coords_pred, coords_true, kind, partners)
    dma = pltpu.SemaphoreType.DMA
    wider = atoms + BAND * TILE
    copy_loss, mean_loss, grad = pl.pallas_call(
        functools.partial(outer_kernel, res, samp),
        name="outer",
        out_shape=(
            jax.ShapeDtypeStruct((copies,), F32),
            jax.ShapeDtypeStruct((1,), F32),
            jax.ShapeDtypeStruct((copies, 3, atoms), F32),
        ),
        in_specs=[vmem] * 7,
        out_specs=(smem, smem, vmem),
        scratch_shapes=[
            pltpu.VMEM((PARTS, wider), F32),
            pltpu.VMEM((copies, 32, wider), BF16),
            pltpu.VMEM((3 * PARTS, atoms), F32),
            *spread,
            pltpu.VMEM((tiles, copies, 8, TILE), F32),
            pltpu.VMEM((2 * (1 + copies), 8, TILE), F32),
            pltpu.VMEM((copies, 3, BAND * TILE), F32),
            pltpu.VMEM((3, BAND * TILE), F32),
            pltpu.VMEM((1, BAND * TILE), jnp.int32),
            pltpu.VMEM((BAND, copies, 8, TILE), F32),
            pltpu.VMEM((BAND, copies, 8, TILE), F32),
            pltpu.VMEM((16, TILE), F32),
            pltpu.VMEM((res, 16, TILE), F32),
            pltpu.VMEM((16, TILE), F32),
            pltpu.VMEM((res, 16, TILE), F32),
            pltpu.VMEM((8, TILE), F32),
            pltpu.VMEM((samp, 8, TILE), F32),
            pltpu.VMEM((6, 16, TILE), F32),
            pltpu.VMEM((copies, 3, atoms), F32),
            dma((3,)),
            dma((3,)),
            dma,
            dma,
            dma((res,)),
            dma((res,)),
            dma((res,)),
            dma((res,)),
            dma((samp,)),
            dma((samp,)),
        ],
        compiler_params=pltpu.CompilerParams(
            collective_id=0, has_side_effects=True, vmem_limit_bytes=VMEM_BYTES
        ),
    )(coords_pred, coords_true, kind, partners, noise_level.reshape(1, copies), inner, inner_sums)
    return (copy_loss, mean_loss.reshape(()), grad)


def solution(mesh):
    in_specs = (P("samp", None, "res"), P(None, "res"), P("res"), P("res", None), P("samp"))
    out_specs = (P("samp"), P(), P("samp", None, "res"))
    body = functools.partial(shards, mesh.shape["res"], mesh.shape["samp"])
    return jax.shard_map(body, mesh=mesh, in_specs=in_specs, out_specs=out_specs, check_vma=False)
```

time: 589 us -> 85.6 us (0.15)
  matrix products: 315 us -> 0 us
  other arithmetic: 139 us -> 0 us
  blocking collectives: 92.3 us -> 0 us
  Pallas kernels: 0 us -> 77.5 us
  local copies, waits for them, and re-layouts: 28 us -> 5.25 us
    dot_general x62 -> x0, matrix products: 315 us -> none  [the longest x18 304 us: pair_terms(): jnp.einsum('skij,skj->si', factor, far_pred[:, component], precision=prec...]
    reduce_sum x9 -> x0, other arithmetic: 92.8 us -> none  [the longest x6 88.8 us: pair_terms(): weight_row = jnp.sum(factor, axis=(1, 3))]
    psum x3 -> x0, blocking collectives: 92.3 us -> none  [the longest x1 34.7 us: shards(): lax.psum((weight_sum, pred_sum, true_sum, cross), 'res')]
    pallas_call x0 -> x2, Pallas kernels: none -> 77.5 us  [the longest x1 51.3 us: shards(): pl.pallas_call(functools.partial(outer_kernel, res, samp), name='outer',...]
    mul x9 -> x0, other arithmetic: 22.7 us -> none  [the longest x6 19.9 us: pair_terms(): score_sum = jnp.sum(mask_fwd * pair_score, axis=(1, 2, 3))]
    gather x18 -> x0, local copies, waits for them, and re-layouts: 15.6 us -> none  [the longest x6 8.85 us: visit_group(): own_rows = jnp.moveaxis(jnp.take(own_tiles, local_ids, axis=1), 1, 0)]
    sub x73 -> x0, local copies, waits for them, and re-layouts: 6.52 us -> none  [the longest x30 4.34 us: pair_terms(): own_pred[:, component, None, :, None] - far_pred[:, component, :, None, :]]
  transfers between devices with their start and end apart: 2 -> 0, of which waited for: 0 -> 0; matrix products, arithmetic and copies ran while one was open for 3% -> 0% of each run, Pallas kernels for 0% -> 0%
where the time goes in v1:
time: 85.6 us; the launch traced here: 85.1 us
  Pallas kernels  77.5 us (91%)
  local copies, waits for them, and re-layouts  5.25 us (6%)
  between operations  2.4 us (3%)
    pallas_call x1, Pallas kernels, shards(): pl.pallas_call(functools.partial(outer_kernel, res, samp), name='outer',...  51.3 us
    pallas_call x1, Pallas kernels, shards(): pl.pallas_call(inner_kernel, name='inner_pairs', out_shape=(jax.ShapeDtyp...  26.2 us
    unnamed x6, local copies, waits for them, and re-layouts  5.25 us

profile of v1, /device:TPU:1, one launch (start us, length us, event | category | flops | bytes accessed | tf_op | source)
XLA Modules:
  0.0 85.1 jit_solution(1872315470134698330)
XLA Ops:
  0.6 1.4 %copy.11.partners = s32[24,5]{1,0:T(8,128)} copy(s32[24,5]{0,1:T(8,128)} %param.8) | data formatting | bytes 960 | tf_op args[3]
  2.0 1.7 %copy.10.pred = f32[4,3,3072]{2,1,0:T(4,128)} copy(f32[4,3,3072]{2,0,1:T(4,128)} %param.5) | data formatting | bytes 294912 | tf_op args[0]
  3.7 26.2 %inner_pairs.1 = (f32[24,4,8,128]{3,2,1,0:T(8,128)}, f32[5,8,128]{2,1,0:T(8,128)}) custom-call(f32[4,3,3072]{2,1,0:T(4,128)} %copy.10.pred, f32[3,3072]{1,0:T(4,128)} %true.3, s32[1,3072]{1,0:T(1,128)} %bitcast.3, s32[24,5]{1,0:T(8,128)} %copy.11.partners), custom_call_target="tpu_custom_call" | custom-call | tf_op jit(solution)/shard_map/inner_pairs/pallas_call | solution.py:529
  29.9 51.3 %outer.1 = (f32[4]{0:T(128)}, f32[1]{0:T(128)}, f32[4,3,3072]{2,1,0:T(4,128)}) custom-call(f32[4,3,3072]{2,1,0:T(4,128)} %copy.10.pred, f32[3,3072]{1,0:T(4,128)} %true.3, s32[1,3072]{1,0:T(1,128)} %bitcast.4, s32[24,5]{1,0:T(8,128)} %copy.11.partners, f32[1,4]{1,0:T(1,128)} %bitcast.5, f32[24,4,8,128]{3,2,1,0:T(8,128)} %get-tuple-element.8.inner, ...), custom_call_target="tpu_custom_call" | custom-call | tf_op jit(solution)/shard_map/outer/pallas_call | solution.py:549
  81.2 0.0 copy-start
  81.2 1.7 %copy.12 = f32[4,3,3072]{2,0,1:T(4,128)} copy(f32[4,3,3072]{2,1,0:T(4,128)} %get-tuple-element.15) | data formatting | bytes 294912
  82.9 0.0 copy-done
  82.9 0.5 copy.15
Async XLA Ops:
  81.2 1.7 %copy-start = (f32[4]{0:T(128)S(1)}, f32[4]{0:T(128)}, u32[]{:S(2)}) copy-start(f32[4]{0:T(128)} %get-tuple-element.19) | copy-start | bytes 52
